TPU v7x, 32 devices: a whole 2x2x4 slice. The times are simulated.
32 devices in a mesh: dp: 8 (over y, x, core), tensor: 4 (over z).
Axes of the slice: x: 2, y: 2, z: 4, core: 2. Of those that a mesh axis runs over, the one named last changes fastest.
Arguments:
- hidden_in: bfloat16 [3, 4096, 768], P(None, ('dp', 'tensor')), may hold values from -6 to 6
- segment_ids: int32 [3, 32, 128], P(None, ('dp', 'tensor')), may hold values from 0 to 7, never falling along the last dimension, each value on 1 to 32 neighbouring positions
- pooled_grad: float32 [3, 32, 8, 768], P(None, ('dp', 'tensor')), may hold values from -96 to 96
- qkv_weight: bfloat16 [3, 768, 768], P(None, 'dp', 'tensor'), may hold values from -0.21875 to 0.21875
- qv_bias: bfloat16 [2, 768], P(None, ('dp', 'tensor')), may hold values from -1.1953125 to 1.1953125
- out_weight: bfloat16 [768, 768], P('tensor', 'dp'), may hold values from -0.875 to 0.875
- out_bias: bfloat16 [768], P(('dp', 'tensor')), may hold values from -1.1953125 to 1.1953125
- norm1_gain: bfloat16 [768], P(('dp', 'tensor')), may hold values from 0.099609375 to 1.8984375
- norm1_shift: bfloat16 [768], P(('dp', 'tensor')), may hold values from -1.1953125 to 1.1953125
- up_weight: bfloat16 [768, 3072], P('dp', 'tensor'), may hold values from -0.21875 to 0.21875
- up_bias: bfloat16 [3072], P(('dp', 'tensor')), may hold values from -1.1953125 to 1.1953125
- down_weight: bfloat16 [3072, 768], P('tensor', 'dp'), may hold values from -0.109375 to 0.109375
- down_bias: bfloat16 [768], P(('dp', 'tensor')), may hold values from -1.1953125 to 1.1953125
- norm2_gain: bfloat16 [768], P(('dp', 'tensor')), may hold values from 0.099609375 to 1.8984375
- norm2_shift: bfloat16 [768], P(('dp', 'tensor')), may hold values from -1.1953125 to 1.1953125
Outputs:
- pooled_out: float32 [3, 32, 8, 768], P(None, ('dp', 'tensor'))
- input_grad: float32 [3, 4096, 768], P(None, ('dp', 'tensor'))
- qkv_weight_grad: float32 [3, 768, 768], P(None, 'dp', 'tensor')
- qv_bias_grad: float32 [2, 768], P(None, ('dp', 'tensor'))
- out_weight_grad: float32 [768, 768], P('tensor', 'dp')
- out_bias_grad: float32 [768], P(('dp', 'tensor'))
- norm1_gain_grad: float32 [768], P(('dp', 'tensor'))
- norm1_shift_grad: float32 [768], P(('dp', 'tensor'))
- up_weight_grad: float32 [768, 3072], P('dp', 'tensor')
- up_bias_grad: float32 [3072], P(('dp', 'tensor'))
- down_weight_grad: float32 [3072, 768], P('tensor', 'dp')
- down_bias_grad: float32 [768], P(('dp', 'tensor'))
- norm2_gain_grad: float32 [768], P(('dp', 'tensor'))
- norm2_shift_grad: float32 [768], P(('dp', 'tensor'))
Inputs may be any that keep to these rules, and one draw needn't show every extreme that they name: `segment_ids`: in every row of 128 tokens the segment numbers never fall, each number from 0 to 7 occurs on 1 to 32 consecutive tokens, and some sentence has exactly 32 tokens.
All inputs are finite; a program needn't handle non-finite values.
Results may differ from a plain program's by a relative error of at most 0.013.
Values may be sent and summed in bfloat16 or wider, within the bound.
No kernel may reach another device: no remote copies, remote signals or barrier semaphores. Data moves between devices by JAX's collectives and lax.ppermute only.
A program may use at most 128 MiB of HBM per device.

v0:
```python
from functools import partial
import jax
import jax.numpy as jnp
from jax import lax
from jax.sharding import PartitionSpec as P

HD = 64
EPS = 1e-12
NEG = -1000000000.0
AXES = ("dp", "tensor")
f32 = jnp.float32
bf16 = jnp.bfloat16


def mm(spec, a, b):
    return jnp.einsum(spec, a, b, preferred_element_type=f32)


def normalize(values, gain, shift):
    center = values - jnp.mean(values, axis=-1, keepdims=True)
    inverse = lax.rsqrt(jnp.mean(center * center, axis=-1, keepdims=True) + EPS)
    normed = center * inverse
    return (normed * gain + shift, normed, inverse)


def normalize_back(grad_out, normed, inverse, gain):
    scaled = grad_out * gain
    return inverse * (
        scaled
        - jnp.mean(scaled, axis=-1, keepdims=True)
        - normed * jnp.mean(scaled * normed, axis=-1, keepdims=True)
    )


def per_device(
    hidden_in,
    segment_ids,
    pooled_grad,
    qkv_weight,
    qv_bias,
    out_weight,
    out_bias,
    norm1_gain,
    norm1_shift,
    up_weight,
    up_bias,
    down_weight,
    down_bias,
    norm2_gain,
    norm2_shift,
):
    n_dp, n_t = (lax.axis_size("dp"), lax.axis_size("tensor"))
    rows = qkv_weight.shape[1]
    hc = qkv_weight.shape[2]
    fc = up_weight.shape[1]
    D = rows * n_dp
    micro, tokens = (hidden_in.shape[0], hidden_in.shape[1])
    seqs, L = (segment_ids.shape[1], segment_ids.shape[2])
    G = micro * seqs
    T = micro * tokens
    segs = pooled_grad.shape[2]
    H = D // HD
    cols = 4 * hc + 2 * fc
    vecs = [
        qv_bias[0],
        qv_bias[1],
        out_bias,
        norm1_gain,
        norm1_shift,
        up_bias,
        down_bias,
        norm2_gain,
        norm2_shift,
    ]
    vlen = [v.shape[0] for v in vecs]
    vec = jnp.concatenate(vecs)
    main = jnp.concatenate(
        [qkv_weight[0], qkv_weight[1], qkv_weight[2], out_weight.T, up_weight, down_weight.T],
        axis=1,
    )
    full = lax.all_gather(main, "dp", axis=0, tiled=True)
    full = lax.all_gather(full, "tensor", axis=0)
    vfull = lax.all_gather(lax.all_gather(vec, "tensor"), "dp").reshape(n_dp * n_t, -1).astype(f32)

    def take(lo, width):
        return full[:, :, lo : lo + width].transpose(1, 0, 2).reshape(D, n_t * width)

    wq, wk, wv, wot = (take(c * hc, hc) for c in range(4))
    wu, wdt = (take(4 * hc, fc), take(4 * hc + fc, fc))
    offs = [0]
    for n in vlen:
        offs.append(offs[-1] + n)
    bq, bv, bo, g1, s1, bu, bd, g2, s2 = (
        vfull[:, offs[j] : offs[j + 1]].reshape(-1) for j in range(9)
    )
    x = hidden_in.reshape(T, D)
    seg = segment_ids.reshape(G, L)
    heads = (G, L, H, HD)
    q = (mm("rd,de->re", x, wq) + bq).astype(bf16).reshape(heads)
    k = mm("rd,de->re", x, wk).astype(bf16).reshape(heads)
    v = (mm("rd,de->re", x, wv) + bv).astype(bf16).reshape(heads)
    scale = float(HD) ** (-0.5)
    same = seg[:, None, :, None] == seg[:, None, None, :]
    s = jnp.where(same, mm("gqhd,gkhd->ghqk", q, k) * scale, NEG)
    e = jnp.exp(s - jnp.max(s, axis=-1, keepdims=True))
    pf = e / jnp.sum(e, axis=-1, keepdims=True)
    pb = pf.astype(bf16)
    o = mm("ghqk,gkhd->gqhd", pb, v).astype(bf16).reshape(T, D)
    a = mm("re,de->rd", o, wot) + bo + x.astype(f32)
    n1, x1, r1 = normalize(a, g1, s1)
    n1b = n1.astype(bf16)
    u = mm("rd,df->rf", n1b, wu) + bu
    z, pull = jax.vjp(partial(jax.nn.gelu, approximate=False), u)
    z = z.astype(bf16)
    b = mm("rf,df->rd", z, wdt) + bd + n1
    y, x2, r2 = normalize(b, g2, s2)
    onehot = (seg[:, :, None] == jnp.arange(segs, dtype=jnp.int32)).astype(f32)
    counts = jnp.sum(onehot, axis=1)
    hi = lax.Precision.HIGHEST
    pooled = (
        jnp.einsum("gls,gld->gsd", onehot, y.reshape(G, L, D), precision=hi) / counts[:, :, None]
    )
    dy = jnp.einsum(
        "gls,gsd->gld", onehot, pooled_grad.reshape(G, segs, D) / counts[:, :, None], precision=hi
    ).reshape(T, D)
    db = normalize_back(dy, x2, r2, g2)
    g_g2, g_s2, g_bd = (jnp.sum(dy * x2, 0), jnp.sum(dy, 0), jnp.sum(db, 0))
    dbb = db.astype(bf16)
    g_wdt = mm("rd,rf->df", dbb, z)
    du = pull(mm("rd,df->rf", dbb, wdt))[0].astype(bf16)
    g_wu = mm("rd,rf->df", n1b, du)
    g_bu = jnp.sum(du.astype(f32), 0)
    dn1 = mm("rf,df->rd", du, wu).astype(bf16).astype(f32) + db
    da = normalize_back(dn1, x1, r1, g1)
    g_g1, g_s1, g_bo = (jnp.sum(dn1 * x1, 0), jnp.sum(dn1, 0), jnp.sum(da, 0))
    dab = da.astype(bf16)
    g_wot = mm("rd,re->de", dab, o)
    do = mm("rd,de->re", dab, wot).astype(bf16).reshape(heads)
    dp = mm("gqhd,gkhd->ghqk", do, v)
    ds = (pf * (dp - jnp.sum(pf * dp, axis=-1, keepdims=True))).astype(bf16)
    dv = mm("ghqk,gqhd->gkhd", pb, do).astype(bf16).reshape(T, D)
    dq = (mm("ghqk,gkhd->gqhd", ds, k) * scale).astype(bf16).reshape(T, D)
    dk = (mm("ghqk,gqhd->gkhd", ds, q) * scale).astype(bf16).reshape(T, D)
    g_q, g_k, g_v = (mm("rd,re->de", x, dd) for dd in (dq, dk, dv))
    g_bq, g_bv = (jnp.sum(dq.astype(f32), 0), jnp.sum(dv.astype(f32), 0))
    dx = mm("re,de->rd", dq, wq) + mm("re,de->rd", dk, wk) + mm("re,de->rd", dv, wv) + da

    def blocks(g):
        return g.astype(bf16).reshape(D, n_t, -1).transpose(1, 0, 2)

    gfull = jnp.concatenate([blocks(g) for g in (g_q, g_k, g_v, g_wot, g_wu, g_wdt)], axis=2)
    gvec = jnp.concatenate(
        [g.reshape(n_dp * n_t, -1) for g in (g_bq, g_bv, g_bo, g_g1, g_s1, g_bu, g_bd, g_g2, g_s2)],
        axis=1,
    )
    gmine = lax.psum_scatter(gfull, "tensor", scatter_dimension=0)
    gmine = lax.psum_scatter(gmine, "dp", scatter_dimension=0, tiled=True).astype(f32)
    gv = lax.psum_scatter(gvec, AXES, scatter_dimension=0)
    vo = [gv[offs[j] : offs[j + 1]] for j in range(9)]
    return (
        pooled.reshape(micro, seqs, segs, D),
        dx.reshape(micro, tokens, D),
        jnp.stack([gmine[:, c * hc : (c + 1) * hc] for c in range(3)]),
        jnp.stack([vo[0], vo[1]]),
        gmine[:, 3 * hc : 4 * hc].T,
        vo[2],
        vo[3],
        vo[4],
        gmine[:, 4 * hc : 4 * hc + fc],
        vo[5],
        gmine[:, 4 * hc + fc :].T,
        vo[6],
        vo[7],
        vo[8],
    )


def solution(mesh):
    both = P(AXES)
    row3 = P(None, AXES)
    return jax.shard_map(
        per_device,
        mesh=mesh,
        in_specs=(
            row3,
            row3,
            row3,
            P(None, "dp", "tensor"),
            row3,
            P("tensor", "dp"),
            both,
            both,
            both,
            P("dp", "tensor"),
            both,
            P("tensor", "dp"),
            both,
            both,
            both,
        ),
        out_specs=(
            row3,
            row3,
            P(None, "dp", "tensor"),
            row3,
            P("tensor", "dp"),
            both,
            both,
            both,
            P("dp", "tensor"),
            both,
            P("tensor", "dp"),
            both,
            both,
            both,
        ),
        check_vma=False,
    )
```

profile of v0, /device:TPU:0, one launch (start us, length us, event | category | flops | bytes accessed | tf_op | source)
XLA Modules:
  0.0 762.0 jit_solution(15456504163924318695)
XLA Ops:
  7.2 0.9 copy.108
  8.1 0.9 slice_bitcast_fusion.11
  9.0 1.9 concatenate.12
  10.9 36.8 %all-gather.7.cloned.1.call-done = bf16[768,2304]{1,0:T(8,128)(2,1)} async-done(((bf16[96,2304]{1,0:T(8,128)(2,1)}), bf16[768,2304]{1,0:T(8,128)(2,1)}) %all-gather.7.cloned.1.call-update) | async-done | bytes 3538960 | tf_op jit(solution)/shard_map/all_gather | solution.py:81
  50.1 11.7 %all-reduce = bf16[1152]{0:T(1024)(128)(2,1)S(1)} all-reduce(bf16[1152]{0:T(1024)(128)(2,1)S(1)} %dynamic-update-slice), channel_id=3, replica_groups=mesh['dp'=8,'tensor'=4] {'tensor'}, use_global_device_ids=true, to_apply=%add | all-reduce | flops 1152 | bytes 4608
  61.8 9.0 %all-gather.3 = bf16[8,4,288]{2,1,0:T(4,128)(2,1)S(1)} all-gather(bf16[1,4,288]{2,1,0:T(4,128)(2,1)S(1)} %reshape.268), channel_id=4, replica_groups=mesh['dp'=8,'tensor'=4] {'dp'}, dimensions={0}, use_global_device_ids=true | all-gather | bytes 20736 | tf_op jit(solution)/shard_map/all_gather | solution.py:83
  74.8 1.3 fusion.84
  76.7 0.7 broadcast_compare_fusion
  77.4 215.8 %all-gather.9.cloned.1.call-done = bf16[3072,2304]{1,0:T(8,128)(2,1)} async-done(((bf16[768,2304]{1,0:T(8,128)(2,1)}), bf16[3072,2304]{1,0:T(8,128)(2,1)}) %all-gather.9.cloned.1.call-update) | async-done | bytes 14155792 | tf_op jit(solution)/shard_map/all_gather | solution.py:82
  293.2 7.3 slice_bitcast_fusion.4
  300.5 7.9 %slice_bitcast_fusion = (bf16[768,4,768]{2,0,1:T(8,128)(2,1)}, bf16[768,4,768]{2,0,1:T(8,128)(2,1)}) fusion(bf16[4,768,2304]{2,1,0:T(8,128)(2,1)} %bitcast.194), kind=kLoop, calls=%fused_computation.7 | loop fusion | bytes 18874368 | tf_op jit(solution)/shard_map/transpose | solution.py:86
  308.4 6.6 copy.119
  315.1 2.6 copy.110
  317.7 2.9 fusion.22
  320.6 2.0 reshape.228
  322.6 2.8 copy.117
  325.3 2.5 copy.111
  327.8 3.0 fusion.17
  330.9 2.6 reshape.230
  333.5 1.5 copy.109
  334.9 2.3 fusion.23
  337.3 1.0 reshape.226
  338.3 2.4 fusion.89
  340.7 2.5 fusion.18
  343.7 0.8 fusion.94
  344.9 0.7 add_rsqrt_fusion.1
  345.6 6.7 copy.118
  352.3 14.5 %multiply_convert_fusion = (bf16[384,3072]{1,0:T(8,128)(2,1)S(1)}, f32[384,3072]{1,0:T(8,128)S(1)}, f32[384,3072]{1,0:T(8,128)S(1)}) fusion(f32[3072]{0:T(1024)} %add.126, bf16[768,3072]{0,1:T(8,128)(2,1)} %bitcast.201, f32[384,768]{1,0:T(8,128)S(1)} %get-tuple-element.119, f32[768]{0:T(1024)} %add.123, f32[768]{0:T(1024)S(1)} %mul.154, ...), kind=kOutput, calls=%fused_computation.11 | convolution fusion | flops 1891270656 | bytes 17716224 | tf_op jit(solution)/shard_map/rd,df->rf/dot_general | solution.py:16
  366.8 5.3 fusion.95
  372.4 1.0 fusion.24
  373.5 2.1 fusion.85
  375.6 7.6 convert_reduce_fusion
  383.2 2.9 multiply_reduce_fusion.1
  386.1 1.0 fusion.86
  387.1 1.5 convolution_convert_fusion.7
  388.6 1.8 convolution_convert_fusion.2
  390.4 1.0 reshape.274
  391.3 1.3 copy.121
  392.7 4.2 convert_reduce_fusion.1
  398.6 1.8 fusion.20
  400.4 1.3 convert_reduce_fusion.2
  401.7 4.8 convolution_convert_fusion.1
  406.5 4.4 convolution_convert_fusion
  410.9 1.8 copy.135
  412.8 1.7 copy.131
  414.5 1.4 copy.128
  415.9 1.4 copy.125
  417.3 1.9 convolution_convert_fusion.3
  419.2 2.6 copy.134
  421.8 3.1 convolution_convert_fusion.4
  424.9 2.5 copy.133
  427.4 3.1 convolution_convert_fusion.5
  430.5 2.5 copy.132
  433.0 8.0 %bitcast_bitcast_fusion = (bf16[4,768,768]{2,1,0:T(8,128)(2,1)}, bf16[4,768,768]{2,1,0:T(8,128)(2,1)}) fusion(bf16[96,4,8,768]{3,2,1,0:T(8,128)(2,1)} %bitcast.207, bf16[96,4,8,768]{3,2,1,0:T(8,128)(2,1)} %bitcast.206), kind=kLoop, calls=%fused_computation.5 | loop fusion | bytes 18874368 | tf_op jit(solution)/shard_map/transpose | solution.py:149
  441.0 21.7 %concatenate.14 = bf16[4,768,2304]{2,1,0:T(8,128)(2,1)} concatenate(bf16[4,768,192]{2,1,0:T(8,128)(2,1)} %bitcast.198, bf16[4,768,192]{2,1,0:T(8,128)(2,1)} %bitcast.197, bf16[4,768,192]{2,1,0:T(8,128)(2,1)} %bitcast.196, bf16[4,768,192]{2,1,0:T(8,128)(2,1)S(1)} %bitcast.195, bf16[4,768,768]{2,1,0:T(8,128)(2,1)} %get-tuple-element.136, bf16[4,768,768]{2,1,0:T(8,128)(2,1)} %get-tuple-element.135), dimensions={2} | concatenate | bytes 28311552 | tf_op jit(solution)/shard_map/concatenate | solution.py:151
  462.8 235.5 %reduce-scatter.3.cloned.1.call-done = bf16[1,768,2304]{2,1,0:T(8,128)(2,1)} async-done(((bf16[4,768,2304]{2,1,0:T(8,128)(2,1)}), bf16[1,768,2304]{2,1,0:T(8,128)(2,1)}) %reduce-scatter.3.cloned.1.call-update) | async-done | bytes 3538960 | tf_op jit(solution)/shard_map/reduce_scatter | solution.py:156
  700.0 41.8 %all-reduce.1 = f32[32,288]{1,0:T(8,128)S(1)} all-reduce(f32[32,288]{1,0:T(8,128)S(1)} %concatenate.15), channel_id=7, replica_groups=mesh['dp'=8,'tensor'=4] {'dp','tensor'}, use_global_device_ids=true, to_apply=%region_23.24.clone | all-reduce | flops 9216 | bytes 73728
  743.5 1.1 fusion.28
  744.7 2.3 fusion.35
  748.3 1.7 fusion.8
  750.1 1.0 reduce-scatter.5.cloned.1.call-done
  751.1 1.1 convert_element_type.162
  753.1 0.7 copy.139
  754.5 0.7 slice.189
  (185 shorter events, 15.4 us)
Async XLA Ops:
  7.2 40.5 %all-gather.7.cloned.1.call-start = ((), (), s32[]{:S(2)}) async-start(), calls=%async_computation.2 | async-start | bytes 3981312 | tf_op jit(solution)/shard_map/all_gather | solution.py:81
  10.9 282.3 %all-gather.9.cloned.1.call-start = ((), (), s32[]{:S(2)}) async-start(), calls=%async_computation.5 | async-start | bytes 17694720 | tf_op jit(solution)/shard_map/all_gather | solution.py:82
  47.7 1.9 copy-start.45
  47.7 1.9 copy-start.47
  47.7 1.9 copy-start.48
  47.7 2.0 copy-start.49
  47.7 1.9 copy-start.50
  47.7 1.9 copy-start.51
  47.8 1.9 copy-start.52
  47.8 1.9 copy-start.53
  47.8 27.0 %copy-start.21 = (f32[3,1,8,768]{3,2,1,0:T(8,128)S(1)}, f32[3,1,8,768]{3,2,1,0:T(8,128)}, u32[]{:S(2)}) copy-start(f32[3,1,8,768]{3,2,1,0:T(8,128)} %param.17) | copy-start | bytes 221188
  47.8 650.5 %reduce-scatter.3.cloned.1.call-start = ((), (), s32[]{:S(2)}) async-start(), calls=%async_computation.3 | async-start | bytes 17694720 | tf_op jit(solution)/shard_map/reduce_scatter | solution.py:156
  71.8 294.9 %copy-start.29 = (f32[768]{0:T(1024)}, f32[768]{0:T(1024)S(1)}, u32[]{:S(2)}) copy-start(f32[768]{0:T(1024)S(1)} %mul.154) | copy-start | bytes 9220
  74.8 218.4 %copy-start.25 = (f32[3,8]{1,0:T(4,128)}, f32[3,8]{1,0:T(4,128)S(1)}, u32[]{:S(2)}) copy-start(f32[3,8]{1,0:T(4,128)S(1)} %convert_reduce_fusion.3) | copy-start | bytes 292
  315.1 2.6 copy-start.54
  322.6 15.7 %copy-start.7 = (bf16[3,128,12,64]{1,0,3,2:T(4,128)(2,1)}, bf16[3,128,12,64]{1,0,3,2:T(4,128)(2,1)S(1)}, u32[]{:S(2)}) copy-start(bf16[3,128,12,64]{1,0,3,2:T(4,128)(2,1)S(1)} %reshape.228) | copy-start | bytes 1769476
  334.9 3.3 copy-start.9
  334.9 3.3 copy-start.22
  340.7 2.5 copy-start.23
  340.7 3.0 copy-start.5
  340.7 3.0 copy-start.55
  343.7 0.9 copy-start.11
  344.6 41.5 %copy-start = (f32[384,768]{1,0:T(8,128)}, f32[384,768]{1,0:T(8,128)S(1)}, u32[]{:S(2)}) copy-start(f32[384,768]{1,0:T(8,128)S(1)} %get-tuple-element.119) | copy-start | bytes 3538948
  352.3 14.5 %copy-start.36 = (f32[384]{0:T(512)S(1)}, f32[384]{0:T(512)}, u32[]{:S(2)}) copy-start(f32[384]{0:T(512)} %add_rsqrt_fusion.1) | copy-start | bytes 4612
  352.3 14.5 %copy-start.40 = (f32[768]{0:T(1024)S(1)}, f32[768]{0:T(1024)}, u32[]{:S(2)}) copy-start(f32[768]{0:T(1024)} %add.123) | copy-start | bytes 9220
  352.3 14.5 %copy-start.44 = (f32[768]{0:T(1024)S(1)}, f32[768]{0:T(1024)}, u32[]{:S(2)}) copy-start(f32[768]{0:T(1024)} %add.129) | copy-start | bytes 9220
  366.8 5.3 copy-start.58
  372.1 1.3 copy-start.34
  372.1 1.3 copy-start.38
  373.5 9.7 %slice-start = ((s8[4718592]{0:T(1024)(128)(4,1)}), s8[4194304]{0:T(1024)(128)(4,1)S(1)}, s32[]{:S(2)}) async-start(s8[4718592]{0:T(1024)(128)(4,1)} %bitcast.202), calls=%async_computation.6 | async-start | bytes 8388608
  375.6 7.6 copy-start.18
  375.6 7.6 slice-start.1
  375.6 7.6 copy-start.30
  383.2 2.9 copy-start.60
  387.1 1.5 copy-start.12
  388.6 1.8 copy-start.16
  391.3 1.3 copy-start.24
  392.7 4.2 copy-start.13
  392.7 4.2 copy-start.20
  397.5 1.1 copy-start.8
  398.6 1.8 copy-start.10
  398.6 3.1 copy-start.61
  400.4 1.3 copy-start.1
  400.4 1.3 copy-start.31
  400.4 1.3 copy-start.37
  400.4 1.3 copy-start.41
  401.7 4.8 copy-start.19
  401.7 4.8 copy-start.59
  412.8 1.7 copy-start.14
  412.8 3.1 copy-start.15
  414.5 2.8 copy-start.56
  462.8 288.3 %reduce-scatter.5.cloned.1.call-start = ((), (), s32[]{:S(2)}) async-start(), calls=%async_computation.4 | async-start | bytes 3981312 | tf_op jit(solution)/shard_map/reduce_scatter | solution.py:157
  698.4 0.9 copy-start.32
  698.4 0.9 copy-start.33
  698.4 1.0 copy-start.43
  698.4 1.1 copy-start.28
  698.4 1.2 copy-start.42
  698.4 1.3 copy-start.39
  698.4 45.1 %copy-start.2 = (f32[384,768]{1,0:T(8,128)S(1)}, f32[384,768]{1,0:T(8,128)}, u32[]{:S(2)}) copy-start(f32[384,768]{1,0:T(8,128)} %get-tuple-element.90) | copy-start | bytes 3538948
  698.4 45.1 %copy-start.26 = (f32[3,8]{1,0:T(4,128)S(1)}, f32[3,8]{1,0:T(4,128)}, u32[]{:S(2)}) copy-start(f32[3,8]{1,0:T(4,128)} %copy-done.25) | copy-start | bytes 292
  744.7 2.3 copy-start.3
  744.7 2.3 copy-start.6
  747.0 1.3 copy-start.4
  751.1 3.5 copy-start.17
  (4 other events, 2.8 us)
Sparse Core Ops, SparseCore 0:
  11.0 36.6 all-gather.6
  49.3 243.9 all-gather.8
  462.9 235.4 reduce-scatter.2
  701.7 49.3 reduce-scatter.4
where the time goes:
time: 773 us; the launch traced here: 762 us
  waiting for transfers between devices  489 us (63%)
  local copies, waits for them, and re-layouts  105 us (14%)
  matrix products  79.7 us (10%)
  blocking collectives  62.4 us (8%)
  between operations  15.4 us (2%)
  other arithmetic  9.89 us (1%)
    reduce_scatter x1, waiting for transfers between devices, per_device(): gmine = lax.psum_scatter(gfull, 'tensor', scatter_dimension=0)  236 us
    all_gather x1, waiting for transfers between devices, per_device(): full = lax.all_gather(full, 'tensor', axis=0)  216 us
    dot_general x23, matrix products, mm(): return jnp.einsum(spec, a, b, preferred_element_type=f32)  74.8 us
    unnamed x2, blocking collectives  53.4 us
    transpose x8, local copies, waits for them, and re-layouts, take(): return full[:, :, lo:lo + width].transpose(1, 0, 2).reshape(D, n_t * width)  37.8 us
    all_gather x1, waiting for transfers between devices, per_device(): full = lax.all_gather(main, 'dp', axis=0, tiled=True)  36.8 us
    concatenate x1, local copies, waits for them, and re-layouts, per_device(): jnp.concatenate([blocks(g) for g in (g_q, g_k, g_v, g_wot, g_wu, g_wdt)],...  21.7 us
  transfers between devices with their start and end apart: 4, of which 4 were waited for; matrix products, arithmetic and copies ran while one was open for 2% of the time, Pallas kernels for 0%

commit v1 on v0

--- a/solution.py
+++ b/solution.py
@@ -10,6 +10,25 @@
 AXES = ("dp", "tensor")
 f32 = jnp.float32
 bf16 = jnp.bfloat16
+
+
+def obtain_trails(field):
+    dev_count = lax.axis_size("dp")
+    all_rows = []
+    for no in range(dev_count):
+        all_rows.append((no, (no + 1) % dev_count))
+
+    def work_pages_over_axis(last):
+        if len(last) == dev_count:
+            return last
+        k_now = work_pages_over_axis([lax.ppermute(last[0], "dp", all_rows), *last])
+        return k_now
+
+    earlier = work_pages_over_axis([field])
+    y2 = jnp.concatenate(earlier, axis=0)
+    front = lax.axis_index("dp")
+    z_new = jnp.roll(y2, (front + 1) * field.shape[0], axis=0)
+    return z_new
 
 
 def mm(spec, a, b):
@@ -78,7 +97,7 @@
         [qkv_weight[0], qkv_weight[1], qkv_weight[2], out_weight.T, up_weight, down_weight.T],
         axis=1,
     )
-    full = lax.all_gather(main, "dp", axis=0, tiled=True)
+    full = obtain_trails(main)
     full = lax.all_gather(full, "tensor", axis=0)
     vfull = lax.all_gather(lax.all_gather(vec, "tensor"), "dp").reshape(n_dp * n_t, -1).astype(f32)
 

time: 773 us -> 794 us (1.027)
  waiting for transfers between devices: 489 us -> 512 us
    ppermute x0 -> x7, waiting for transfers between devices: none -> 60.6 us  [work_pages_over_axis(): k_now = work_pages_over_axis([lax.ppermute(last[0], 'dp', all_rows), *last])]
    all_gather x1 -> x0, waiting for transfers between devices: 36.8 us -> none  [per_device(): full = lax.all_gather(main, 'dp', axis=0, tiled=True)]
  transfers between devices with their start and end apart: 4 -> 10, of which waited for: 4 -> 10; matrix products, arithmetic and copies ran while one was open for 2% -> 2% of each run, Pallas kernels for 0% -> 0%
where the time goes in v1:
time: 794 us; the launch traced here: 789 us
  waiting for transfers between devices  512 us (64%)
  local copies, waits for them, and re-layouts  108 us (14%)
  matrix products  79.6 us (10%)
  blocking collectives  63.8 us (8%)
  between operations  15.6 us (2%)
  other arithmetic  9.82 us (1%)
    reduce_scatter x1, waiting for transfers between devices, per_device(): gmine = lax.psum_scatter(gfull, 'tensor', scatter_dimension=0)  235 us
    all_gather x1, waiting for transfers between devices, per_device(): full = lax.all_gather(full, 'tensor', axis=0)  214 us
    dot_general x23, matrix products, mm(): return jnp.einsum(spec, a, b, preferred_element_type=f32)  74.7 us
    ppermute x7, waiting for transfers between devices, work_pages_over_axis(): k_now = work_pages_over_axis([lax.ppermute(last[0], 'dp', all_rows), *last])  60.6 us
    unnamed x2, blocking collectives  54.5 us
    transpose x8, local copies, waits for them, and re-layouts, take(): return full[:, :, lo:lo + width].transpose(1, 0, 2).reshape(D, n_t * width)  37.7 us
    concatenate x1, local copies, waits for them, and re-layouts, per_device(): jnp.concatenate([blocks(g) for g in (g_q, g_k, g_v, g_wot, g_wu, g_wdt)],...  21.8 us
  transfers between devices with their start and end apart: 10, of which 10 were waited for; matrix products, arithmetic and copies ran while one was open for 2% of the time, Pallas kernels for 0%

profile of v1, /device:TPU:0, one launch (start us, length us, event | category | flops | bytes accessed | tf_op | source)
XLA Modules:
  0.0 789.4 jit_solution(1369196902616025391)
XLA Ops:
  9.0 1.1 concatenate.18
  10.6 8.9 %collective-permute-done = bf16[96,2304]{1,0:T(8,128)(2,1)S(1)} collective-permute-done((bf16[96,2304]{1,0:T(8,128)(2,1)S(1)}, bf16[96,2304]{1,0:T(8,128)(2,1)S(1)}, u32[]{:S(2)}, u32[]{:S(2)}) %collective-permute-start) | collective-permute-done | bytes 442400 | tf_op jit(solution)/shard_map/ppermute | solution.py:24
  19.5 8.6 %collective-permute-done.1 = bf16[96,2304]{1,0:T(8,128)(2,1)S(1)} collective-permute-done((bf16[96,2304]{1,0:T(8,128)(2,1)S(1)}, bf16[96,2304]{1,0:T(8,128)(2,1)S(1)}, u32[]{:S(2)}, u32[]{:S(2)}) %collective-permute-start.1) | collective-permute-done | bytes 442400 | tf_op jit(solution)/shard_map/ppermute | solution.py:24
  28.1 8.6 %collective-permute-done.2 = bf16[96,2304]{1,0:T(8,128)(2,1)S(1)} collective-permute-done((bf16[96,2304]{1,0:T(8,128)(2,1)S(1)}, bf16[96,2304]{1,0:T(8,128)(2,1)S(1)}, u32[]{:S(2)}, u32[]{:S(2)}) %collective-permute-start.2) | collective-permute-done | bytes 442400 | tf_op jit(solution)/shard_map/ppermute | solution.py:24
  36.7 8.6 %collective-permute-done.3 = bf16[96,2304]{1,0:T(8,128)(2,1)S(1)} collective-permute-done((bf16[96,2304]{1,0:T(8,128)(2,1)S(1)}, bf16[96,2304]{1,0:T(8,128)(2,1)S(1)}, u32[]{:S(2)}, u32[]{:S(2)}) %collective-permute-start.3) | collective-permute-done | bytes 442400 | tf_op jit(solution)/shard_map/ppermute | solution.py:24
  45.4 8.6 %collective-permute-done.4 = bf16[96,2304]{1,0:T(8,128)(2,1)S(1)} collective-permute-done((bf16[96,2304]{1,0:T(8,128)(2,1)S(1)}, bf16[96,2304]{1,0:T(8,128)(2,1)S(1)}, u32[]{:S(2)}, u32[]{:S(2)}) %collective-permute-start.4) | collective-permute-done | bytes 442400 | tf_op jit(solution)/shard_map/ppermute | solution.py:24
  54.0 8.6 %collective-permute-done.5 = bf16[96,2304]{1,0:T(8,128)(2,1)S(1)} collective-permute-done((bf16[96,2304]{1,0:T(8,128)(2,1)S(1)}, bf16[96,2304]{1,0:T(8,128)(2,1)S(1)}, u32[]{:S(2)}, u32[]{:S(2)}) %collective-permute-start.5) | collective-permute-done | bytes 442400 | tf_op jit(solution)/shard_map/ppermute | solution.py:24
  62.6 8.6 %collective-permute-done.6 = bf16[96,2304]{1,0:T(8,128)(2,1)S(1)} collective-permute-done((bf16[96,2304]{1,0:T(8,128)(2,1)S(1)}, bf16[96,2304]{1,0:T(8,128)(2,1)S(1)}, u32[]{:S(2)}, u32[]{:S(2)}) %collective-permute-start.6) | collective-permute-done | bytes 442400 | tf_op jit(solution)/shard_map/ppermute | solution.py:24
  71.9 2.6 constant_dynamic-slice_fusion.1
  76.8 12.7 %all-reduce = bf16[1152]{0:T(1024)(128)(2,1)S(1)} all-reduce(bf16[1152]{0:T(1024)(128)(2,1)S(1)} %dynamic-update-slice), channel_id=3, replica_groups=mesh['dp'=8,'tensor'=4] {'tensor'}, use_global_device_ids=true, to_apply=%add | all-reduce | flops 1152 | bytes 4608
  89.6 9.3 %all-gather.3 = bf16[8,4,288]{2,1,0:T(4,128)(2,1)S(1)} all-gather(bf16[1,4,288]{2,1,0:T(4,128)(2,1)S(1)} %reshape.268), channel_id=4, replica_groups=mesh['dp'=8,'tensor'=4] {'dp'}, dimensions={0}, use_global_device_ids=true | all-gather | bytes 20736 | tf_op jit(solution)/shard_map/all_gather | solution.py:102
  102.9 1.3 fusion.84
  105.5 214.2 %all-gather.6.cloned.1.call-done = bf16[3072,2304]{1,0:T(8,128)(2,1)} async-done(((bf16[768,2304]{1,0:T(8,128)(2,1)}), bf16[3072,2304]{1,0:T(8,128)(2,1)}) %all-gather.6.cloned.1.call-update) | async-done | bytes 14155792 | tf_op jit(solution)/shard_map/all_gather | solution.py:101
  319.7 7.2 slice_bitcast_fusion.4
  327.0 7.9 %slice_bitcast_fusion = (bf16[768,4,768]{2,0,1:T(8,128)(2,1)}, bf16[768,4,768]{2,0,1:T(8,128)(2,1)}) fusion(bf16[4,768,2304]{2,1,0:T(8,128)(2,1)} %bitcast.194), kind=kLoop, calls=%fused_computation.7 | loop fusion | bytes 18874368 | tf_op jit(solution)/shard_map/transpose | solution.py:105
  334.9 6.7 copy.119
  341.5 2.6 copy.110
  344.1 2.9 fusion.22
  347.0 2.0 reshape.228
  349.0 2.8 copy.117
  351.8 2.5 copy.111
  354.3 3.0 fusion.17
  357.3 2.6 reshape.230
  359.9 1.5 copy.109
  361.4 2.3 fusion.23
  363.7 1.0 reshape.226
  364.7 2.4 fusion.89
  367.1 2.5 fusion.18
  371.9 6.6 copy.118
  378.5 14.5 %multiply_convert_fusion = (bf16[384,3072]{1,0:T(8,128)(2,1)S(1)}, f32[384,3072]{1,0:T(8,128)S(1)}, f32[384,3072]{1,0:T(8,128)S(1)}) fusion(f32[3072]{0:T(1024)} %add.142, bf16[768,3072]{0,1:T(8,128)(2,1)} %bitcast.201, f32[384,768]{1,0:T(8,128)S(1)} %get-tuple-element.119, f32[768]{0:T(1024)} %add.139, f32[768]{0:T(1024)S(1)} %mul.158, ...), kind=kOutput, calls=%fused_computation.11 | convolution fusion | flops 1891270656 | bytes 17716224 | tf_op jit(solution)/shard_map/rd,df->rf/dot_general | solution.py:35
  393.1 5.3 fusion.95
  398.7 1.0 fusion.24
  399.8 2.1 fusion.85
  401.9 7.6 convert_reduce_fusion
  409.5 2.9 multiply_reduce_fusion.1
  412.4 1.0 fusion.86
  413.4 1.5 convolution_convert_fusion.7
  414.9 1.8 convolution_convert_fusion.2
  416.7 1.0 reshape.274
  417.7 1.3 copy.121
  419.0 4.2 convert_reduce_fusion.1
  425.0 1.7 fusion.20
  426.7 1.3 convert_reduce_fusion.2
  428.0 4.8 convolution_convert_fusion.1
  432.8 4.4 convolution_convert_fusion
  437.2 1.8 copy.135
  439.1 1.7 copy.131
  440.8 2.5 copy.128
  443.2 1.4 copy.125
  444.7 1.9 convolution_convert_fusion.3
  446.5 2.6 copy.134
  449.1 3.1 convolution_convert_fusion.4
  452.2 2.5 copy.133
  454.8 3.1 convolution_convert_fusion.5
  457.9 2.5 copy.132
  460.4 8.0 %bitcast_bitcast_fusion = (bf16[4,768,768]{2,1,0:T(8,128)(2,1)}, bf16[4,768,768]{2,1,0:T(8,128)(2,1)}) fusion(bf16[96,4,8,768]{3,2,1,0:T(8,128)(2,1)} %bitcast.207, bf16[96,4,8,768]{3,2,1,0:T(8,128)(2,1)} %bitcast.206), kind=kLoop, calls=%fused_computation.5 | loop fusion | bytes 18874368 | tf_op jit(solution)/shard_map/transpose | solution.py:168
  468.4 21.8 %concatenate.21 = bf16[4,768,2304]{2,1,0:T(8,128)(2,1)} concatenate(bf16[4,768,192]{2,1,0:T(8,128)(2,1)} %bitcast.198, bf16[4,768,192]{2,1,0:T(8,128)(2,1)} %bitcast.197, bf16[4,768,192]{2,1,0:T(8,128)(2,1)} %bitcast.196, bf16[4,768,192]{2,1,0:T(8,128)(2,1)S(1)} %bitcast.195, bf16[4,768,768]{2,1,0:T(8,128)(2,1)} %get-tuple-element.136, bf16[4,768,768]{2,1,0:T(8,128)(2,1)} %get-tuple-element.135), dimensions={2} | concatenate | bytes 28311552 | tf_op jit(solution)/shard_map/concatenate | solution.py:170
  490.3 235.4 %reduce-scatter.3.cloned.1.call-done = bf16[1,768,2304]{2,1,0:T(8,128)(2,1)} async-done(((bf16[4,768,2304]{2,1,0:T(8,128)(2,1)}), bf16[1,768,2304]{2,1,0:T(8,128)(2,1)}) %reduce-scatter.3.cloned.1.call-update) | async-done | bytes 3538960 | tf_op jit(solution)/shard_map/reduce_scatter | solution.py:175
  726.7 41.8 %all-reduce.1 = f32[32,288]{1,0:T(8,128)S(1)} all-reduce(f32[32,288]{1,0:T(8,128)S(1)} %concatenate.22), channel_id=7, replica_groups=mesh['dp'=8,'tensor'=4] {'dp','tensor'}, use_global_device_ids=true, to_apply=%region_23.24.clone | all-reduce | flops 9216 | bytes 73728
  770.3 1.1 fusion.28
  771.5 2.2 fusion.35
  774.9 1.7 fusion.8
  776.7 1.8 reduce-scatter.5.cloned.1.call-done
  778.5 1.1 convert_element_type.162
  (211 shorter events, 21.1 us)
Async XLA Ops:
  7.2 312.5 %all-gather.6.cloned.1.call-start = ((), (), s32[]{:S(2)}) async-start(), calls=%async_computation.4 | async-start | bytes 17694720 | tf_op jit(solution)/shard_map/all_gather | solution.py:101
  10.1 9.4 %collective-permute-start = (bf16[96,2304]{1,0:T(8,128)(2,1)S(1)}, bf16[96,2304]{1,0:T(8,128)(2,1)S(1)}, u32[]{:S(2)}, u32[]{:S(2)}) collective-permute-start(bf16[96,2304]{1,0:T(8,128)(2,1)S(1)} %concatenate.18), channel_id=1, source_target_pairs={{0,4},{4,8},{8,12},{12,16},{16,20},{20,24},{24,28},{28,0},{1,5},{5... | collective-permute-start | bytes 1327112 | tf_op jit(solution)/shard_map/ppermute | solution.py:24
  19.5 8.6 %collective-permute-start.1 = (bf16[96,2304]{1,0:T(8,128)(2,1)S(1)}, bf16[96,2304]{1,0:T(8,128)(2,1)S(1)}, u32[]{:S(2)}, u32[]{:S(2)}) collective-permute-start(bf16[96,2304]{1,0:T(8,128)(2,1)S(1)} %collective-permute-done), channel_id=1, source_target_pairs={{0,4},{4,8},{8,12},{12,16},{16,20},{20,24},{24,28},{28,0},{1,5},{5... | collective-permute-start | bytes 1327112 | tf_op jit(solution)/shard_map/ppermute | solution.py:24
  28.1 8.6 %collective-permute-start.2 = (bf16[96,2304]{1,0:T(8,128)(2,1)S(1)}, bf16[96,2304]{1,0:T(8,128)(2,1)S(1)}, u32[]{:S(2)}, u32[]{:S(2)}) collective-permute-start(bf16[96,2304]{1,0:T(8,128)(2,1)S(1)} %collective-permute-done.1), channel_id=1, source_target_pairs={{0,4},{4,8},{8,12},{12,16},{16,20},{20,24},{24,28},{28,0},{1,5},{5... | collective-permute-start | bytes 1327112 | tf_op jit(solution)/shard_map/ppermute | solution.py:24
  36.7 8.6 %collective-permute-start.3 = (bf16[96,2304]{1,0:T(8,128)(2,1)S(1)}, bf16[96,2304]{1,0:T(8,128)(2,1)S(1)}, u32[]{:S(2)}, u32[]{:S(2)}) collective-permute-start(bf16[96,2304]{1,0:T(8,128)(2,1)S(1)} %collective-permute-done.2), channel_id=1, source_target_pairs={{0,4},{4,8},{8,12},{12,16},{16,20},{20,24},{24,28},{28,0},{1,5},{5... | collective-permute-start | bytes 1327112 | tf_op jit(solution)/shard_map/ppermute | solution.py:24
  45.3 8.6 %collective-permute-start.4 = (bf16[96,2304]{1,0:T(8,128)(2,1)S(1)}, bf16[96,2304]{1,0:T(8,128)(2,1)S(1)}, u32[]{:S(2)}, u32[]{:S(2)}) collective-permute-start(bf16[96,2304]{1,0:T(8,128)(2,1)S(1)} %collective-permute-done.3), channel_id=1, source_target_pairs={{0,4},{4,8},{8,12},{12,16},{16,20},{20,24},{24,28},{28,0},{1,5},{5... | collective-permute-start | bytes 1327112 | tf_op jit(solution)/shard_map/ppermute | solution.py:24
  54.0 8.6 %collective-permute-start.5 = (bf16[96,2304]{1,0:T(8,128)(2,1)S(1)}, bf16[96,2304]{1,0:T(8,128)(2,1)S(1)}, u32[]{:S(2)}, u32[]{:S(2)}) collective-permute-start(bf16[96,2304]{1,0:T(8,128)(2,1)S(1)} %collective-permute-done.4), channel_id=1, source_target_pairs={{0,4},{4,8},{8,12},{12,16},{16,20},{20,24},{24,28},{28,0},{1,5},{5... | collective-permute-start | bytes 1327112 | tf_op jit(solution)/shard_map/ppermute | solution.py:24
  62.6 8.6 %collective-permute-start.6 = (bf16[96,2304]{1,0:T(8,128)(2,1)S(1)}, bf16[96,2304]{1,0:T(8,128)(2,1)S(1)}, u32[]{:S(2)}, u32[]{:S(2)}) collective-permute-start(bf16[96,2304]{1,0:T(8,128)(2,1)S(1)} %collective-permute-done.5), channel_id=1, source_target_pairs={{0,4},{4,8},{8,12},{12,16},{16,20},{20,24},{24,28},{28,0},{1,5},{5... | collective-permute-start | bytes 1327112 | tf_op jit(solution)/shard_map/ppermute | solution.py:24
  74.5 1.9 copy-start.44
  74.5 1.9 copy-start.46
  74.5 1.9 copy-start.47
  74.5 1.9 copy-start.48
  74.5 1.9 copy-start.49
  74.5 1.9 copy-start.50
  74.5 1.9 copy-start.51
  74.5 1.9 copy-start.52
  74.5 28.4 %copy-start.20 = (f32[3,1,8,768]{3,2,1,0:T(8,128)S(1)}, f32[3,1,8,768]{3,2,1,0:T(8,128)}, u32[]{:S(2)}) copy-start(f32[3,1,8,768]{3,2,1,0:T(8,128)} %param.17) | copy-start | bytes 221188
  74.6 651.2 %reduce-scatter.3.cloned.1.call-start = ((), (), s32[]{:S(2)}) async-start(), calls=%async_computation.2 | async-start | bytes 17694720 | tf_op jit(solution)/shard_map/reduce_scatter | solution.py:175
  100.0 293.1 %copy-start.28 = (f32[768]{0:T(1024)}, f32[768]{0:T(1024)S(1)}, u32[]{:S(2)}) copy-start(f32[768]{0:T(1024)S(1)} %mul.158) | copy-start | bytes 9220
  102.9 216.8 %copy-start.24 = (f32[3,8]{1,0:T(4,128)}, f32[3,8]{1,0:T(4,128)S(1)}, u32[]{:S(2)}) copy-start(f32[3,8]{1,0:T(4,128)S(1)} %convert_reduce_fusion.3) | copy-start | bytes 292
  341.5 2.6 copy-start.53
  349.0 15.7 %copy-start.7 = (bf16[3,128,12,64]{1,0,3,2:T(4,128)(2,1)}, bf16[3,128,12,64]{1,0,3,2:T(4,128)(2,1)S(1)}, u32[]{:S(2)}) copy-start(bf16[3,128,12,64]{1,0,3,2:T(4,128)(2,1)S(1)} %reshape.228) | copy-start | bytes 1769476
  361.4 3.3 copy-start.9
  361.4 3.3 copy-start.21
  367.1 2.5 copy-start.22
  367.1 3.0 copy-start.5
  367.1 3.0 copy-start.54
  370.9 41.5 %copy-start = (f32[384,768]{1,0:T(8,128)}, f32[384,768]{1,0:T(8,128)S(1)}, u32[]{:S(2)}) copy-start(f32[384,768]{1,0:T(8,128)S(1)} %get-tuple-element.119) | copy-start | bytes 3538948
  378.5 14.6 %copy-start.35 = (f32[384]{0:T(512)S(1)}, f32[384]{0:T(512)}, u32[]{:S(2)}) copy-start(f32[384]{0:T(512)} %add_rsqrt_fusion.1) | copy-start | bytes 4612
  378.5 14.6 %copy-start.39 = (f32[768]{0:T(1024)S(1)}, f32[768]{0:T(1024)}, u32[]{:S(2)}) copy-start(f32[768]{0:T(1024)} %add.139) | copy-start | bytes 9220
  378.5 14.6 %copy-start.43 = (f32[768]{0:T(1024)S(1)}, f32[768]{0:T(1024)}, u32[]{:S(2)}) copy-start(f32[768]{0:T(1024)} %add.145) | copy-start | bytes 9220
  393.1 5.3 copy-start.57
  399.8 9.7 %slice-start = ((s8[4718592]{0:T(1024)(128)(4,1)}), s8[4194304]{0:T(1024)(128)(4,1)S(1)}, s32[]{:S(2)}) async-start(s8[4718592]{0:T(1024)(128)(4,1)} %bitcast.202), calls=%async_computation.5 | async-start | bytes 8388608
  401.9 7.6 copy-start.17
  401.9 7.6 slice-start.1
  401.9 7.6 copy-start.29
  409.5 2.9 copy-start.59
  414.9 1.8 copy-start.15
  416.7 2.3 copy-start.23
  419.0 4.2 copy-start.13
  419.0 4.2 copy-start.19
  425.0 3.0 copy-start.1
  425.0 3.0 copy-start.30
  425.0 3.0 copy-start.36
  425.0 3.0 copy-start.40
  425.0 3.0 copy-start.60
  428.0 4.8 copy-start.18
  428.0 4.8 copy-start.58
  439.1 4.2 copy-start.14
  439.1 5.6 copy-start.55
  490.2 235.6 %copy-start.26 = (f32[768]{0:T(1024)S(1)}, f32[768]{0:T(1024)}, u32[]{:S(2)}) copy-start(f32[768]{0:T(1024)} %get-tuple-element.75) | copy-start | bytes 9220
  490.2 235.7 %copy-start.34 = (f32[3072]{0:T(1024)S(1)}, f32[3072]{0:T(1024)}, u32[]{:S(2)}) copy-start(f32[3072]{0:T(1024)} %get-tuple-element.131) | copy-start | bytes 36868
  490.2 235.8 %copy-start.31 = (f32[768]{0:T(1024)S(1)}, f32[768]{0:T(1024)}, u32[]{:S(2)}) copy-start(f32[768]{0:T(1024)} %get-tuple-element.80) | copy-start | bytes 9220
  490.2 235.9 %copy-start.32 = (f32[768]{0:T(1024)S(1)}, f32[768]{0:T(1024)}, u32[]{:S(2)}) copy-start(f32[768]{0:T(1024)} %get-tuple-element.78) | copy-start | bytes 9220
  490.2 236.0 %copy-start.42 = (f32[768]{0:T(1024)S(1)}, f32[768]{0:T(1024)}, u32[]{:S(2)}) copy-start(f32[768]{0:T(1024)} %get-tuple-element.72) | copy-start | bytes 9220
  490.2 236.0 %copy-start.27 = (f32[768]{0:T(1024)S(1)}, f32[768]{0:T(1024)}, u32[]{:S(2)}) copy-start(f32[768]{0:T(1024)} %get-tuple-element.70) | copy-start | bytes 9220
  490.2 236.1 %copy-start.41 = (f32[768]{0:T(1024)S(1)}, f32[768]{0:T(1024)}, u32[]{:S(2)}) copy-start(f32[768]{0:T(1024)} %get-tuple-element.77) | copy-start | bytes 9220
  490.2 236.2 %copy-start.38 = (f32[12,64]{1,0:T(8,128)S(1)}, f32[12,64]{1,0:T(8,128)}, u32[]{:S(2)}) copy-start(f32[12,64]{1,0:T(8,128)} %get-tuple-element.129) | copy-start | bytes 9220
  490.3 280.1 %copy-start.2 = (f32[384,768]{1,0:T(8,128)S(1)}, f32[384,768]{1,0:T(8,128)}, u32[]{:S(2)}) copy-start(f32[384,768]{1,0:T(8,128)} %get-tuple-element.90) | copy-start | bytes 3538948
  490.3 280.1 %copy-start.25 = (f32[3,8]{1,0:T(4,128)S(1)}, f32[3,8]{1,0:T(4,128)}, u32[]{:S(2)}) copy-start(f32[3,8]{1,0:T(4,128)} %copy-done.24) | copy-start | bytes 292
  490.3 288.2 %reduce-scatter.5.cloned.1.call-start = ((), (), s32[]{:S(2)}) async-start(), calls=%async_computation.3 | async-start | bytes 3981312 | tf_op jit(solution)/shard_map/reduce_scatter | solution.py:176
  770.3 3.3 copy-start.3
  770.3 3.3 copy-start.6
  778.5 3.5 copy-start.16
  (9 other events, 10.8 us)
Sparse Core Ops, SparseCore 0:
  74.7 244.9 all-gather.5
  490.3 235.4 reduce-scatter.2
  729.2 49.1 reduce-scatter.4
